TPU v7x, 128 devices: a whole 4x4x4 slice. The times are simulated.
128 devices in a mesh: gz: 16 (over z_hi, x, core), xy: 8 (over z_lo, y).
Axes of the slice: x: 4, y: 4, z: 4 (z_hi: 2, z_lo: 2; z = z_hi * 2 + z_lo), core: 2. Of those that a mesh axis runs over, the one named last changes fastest.
Arguments:
- prior_estimate: float32 [768, 256, 128], P('gz', 'xy'), may hold values from 0.5 to 2
- views_upright: float32 [3, 768, 256, 128], P(None, 'gz', 'xy'), may hold values from 0.2 to 5
- views_turned: float32 [3, 768, 128, 256], P(None, 'gz', 'xy'), may hold values from 0.2 to 5
- kernel_depth: float32 [6, 61], replicated, may hold values from 0.005 to 1.55, as said below
- kernel_rows: float32 [6, 31], replicated, may hold values from 0.005 to 1.55, as said below
- kernel_columns: float32 [6, 31], replicated, may hold values from 0.005 to 1.55, as said below
- lateral_offsets: int32 [6], replicated, may hold values from -8 to 8, as said below
- block_views: int32 [128, 3], replicated, may hold values from 0 to 5, all different within a row
Outputs:
- estimate: float32 [768, 256, 128], P('gz', 'xy')
Inputs may be any that keep to these rules, and one draw needn't show every extreme that they name: `block_views`: row r holds 3 different views and belongs to the block at position r // 8 along gz and r % 8 along xy. `lateral_offsets`: one view has offset 8 and another -8. `kernel_depth`: positive taps. `kernel_rows`: positive taps. `kernel_columns`: positive taps.
All inputs are finite; a program needn't handle non-finite values.
Results may differ from a plain program's by a relative error of at most 0.00005.
Values sent between devices are 32-bit elements; how exact they have to be, the bound alone decides.
A program may use at most 128 MiB of HBM per device.

v0:
```python
import jax
import jax.numpy as jnp
from jax import lax
from jax.sharding import PartitionSpec as P

ITERS = 2
exact_mode = lax.Precision.HIGHEST


def padded(cells, sides, width):
    for axis, dim in sides:
        count = lax.axis_size(axis)
        ends = count - 1
        head = lax.slice_in_dim(cells, 0, width, axis=dim)
        tail = lax.slice_in_dim(cells, cells.shape[dim] - width, cells.shape[dim], axis=dim)
        cells = jnp.concatenate(
            [
                lax.ppermute(tail, axis, [(i, (i + 1) % count) for i in range(ends)]),
                cells,
                lax.ppermute(head, axis, [((i + 1) % count, i) for i in range(ends)]),
            ],
            axis=dim,
        )
    return cells


def band_matrix(kernel, length):
    extent = kernel.shape[0]
    row_index = jnp.arange(length, dtype=jnp.int32)[:, None]
    col_index = jnp.arange(length + extent - 1, dtype=jnp.int32)[None, :]
    offset = col_index - row_index
    choose = (offset[:, :, None] == jnp.arange(extent, dtype=jnp.int32)[None, None, :]).astype(
        jnp.float32
    )
    return jnp.sum(choose * kernel[None, None, :], axis=2)


def lateral_matrix(kernel, displacement, length):
    extent = kernel.shape[0]
    radius = (extent - 1) // 2
    row_index = jnp.arange(length, dtype=jnp.int32)[:, None]
    col_index = jnp.arange(length, dtype=jnp.int32)[None, :]
    offset = col_index - row_index + radius + displacement
    choose = (offset[:, :, None] == jnp.arange(extent, dtype=jnp.int32)[None, None, :]).astype(
        jnp.float32
    )
    return jnp.sum(choose * kernel[None, None, :], axis=2)


def normalize(kernel):
    return kernel / jnp.sum(kernel, axis=-1, keepdims=True)


def blur_forward(haloed, band_depth, band_rows, lateral):
    section = jnp.einsum("zj,jyx->zyx", band_depth, haloed, precision=exact_mode)
    section = jnp.einsum("yj,zjx->zyx", band_rows, section, precision=exact_mode)
    return jnp.einsum("zyj,xj->zyx", section, lateral, precision=exact_mode)


def local(
    prior_estimate,
    views_upright,
    views_turned,
    kernel_depth,
    kernel_rows,
    kernel_columns,
    lateral_offsets,
    block_views,
):
    depth, rows, columns = prior_estimate.shape
    count_views = kernel_depth.shape[0]
    count_blocks = block_views.shape[0]
    count_active = block_views.shape[1]
    reach_depth = (kernel_depth.shape[1] - 1) // 2
    reach_rows = (kernel_rows.shape[1] - 1) // 2
    turned = jnp.transpose(
        lax.all_to_all(views_turned, "xy", split_axis=3, concat_axis=2, tiled=True), (0, 1, 3, 2)
    )
    observed = jnp.concatenate([views_upright, turned], axis=0)
    taps_depth = normalize(kernel_depth)
    taps_rows = normalize(kernel_rows)
    taps_columns = normalize(kernel_columns)
    forward_depth = [band_matrix(taps_depth[number], depth) for number in range(count_views)]
    forward_rows = [band_matrix(taps_rows[number], rows) for number in range(count_views)]
    laterals = [
        lateral_matrix(taps_columns[number], lateral_offsets[number], columns)
        for number in range(count_views)
    ]
    member = (
        jnp.sum(
            (
                block_views[:, :, None] == jnp.arange(count_views, dtype=jnp.int32)[None, None, :]
            ).astype(jnp.float32),
            axis=1,
        )
        / count_active
    )
    side_count = lax.axis_size("xy")
    here_depth = lax.axis_index("gz")
    here_rows = lax.axis_index("xy")
    block_list = jnp.arange(count_blocks, dtype=jnp.int32)
    own_id = here_depth * side_count + here_rows
    picker = (block_list == own_id).astype(jnp.float32)
    own_weights = jnp.dot(picker, member, precision=exact_mode)
    adjoint_depth = [band_matrix(taps_depth[number][::-1], depth) for number in range(count_views)]
    adjoint_rows = [band_matrix(taps_rows[number][::-1], rows) for number in range(count_views)]
    estimate = prior_estimate
    for iteration in range(ITERS):
        haloed = padded(estimate, (("xy", 1),), reach_rows)
        haloed = padded(haloed, (("gz", 0),), reach_depth)
        correction = jnp.zeros_like(estimate)
        for number in range(count_views):
            blurred = blur_forward(
                haloed, forward_depth[number], forward_rows[number], laterals[number]
            )
            quotient = observed[number] / blurred
            rimmed = padded(quotient, (("xy", 1),), reach_rows)
            rimmed = padded(rimmed, (("gz", 0),), reach_depth)
            back = jnp.einsum("zj,jyx->zyx", adjoint_depth[number], rimmed, precision=exact_mode)
            back = jnp.einsum("yj,zjx->zyx", adjoint_rows[number], back, precision=exact_mode)
            back = jnp.einsum("zyj,jx->zyx", back, laterals[number], precision=exact_mode)
            correction = correction + own_weights[number] * back
        estimate = estimate * correction
    return estimate


def solution(mesh):
    in_specs = (
        P("gz", "xy", None),
        P(None, "gz", "xy", None),
        P(None, "gz", "xy", None),
        P(),
        P(),
        P(),
        P(),
        P(),
    )
    out_specs = P("gz", "xy", None)
    return jax.shard_map(local, mesh=mesh, in_specs=in_specs, out_specs=out_specs, check_vma=False)
```

profile of v0, /device:TPU:31, one launch (start us, length us, event | category | flops | bytes accessed | tf_op | source)
XLA Modules:
  0.0 543.5 jit_solution(17599730964510681161)
XLA Ops:
  7.6 5.5 %copy.134 = f32[3,48,16,256]{1,2,0,3:T(8,128)} copy(f32[3,48,16,256]{3,2,1,0:T(8,128)S(1)} %copy-done.8) | data formatting | bytes 4718592 | tf_op args[2]
  13.1 9.5 %reshape.154 = f32[8,1,73728]{2,1,0:T(1,128)} reshape(f32[256,3,16,48]{3,2,1,0:T(8,128)} %bitcast.336) | data formatting | bytes 4718592
  22.6 6.2 %all-to-all-start = ((f32[8,1,73728]{2,1,0:T(1,128)}), f32[8,1,73728]{2,1,0:T(1,128)S(1)}, u32[]{:S(2)}, u32[]{:S(2)}) async-start(f32[8,1,73728]{2,1,0:T(1,128)} %reshape.154), calls=%async_computation | async-start | bytes 4718592 | tf_op jit(solution)/shard_map/all_to_all | solution.py:77
  69.8 5.6 %collective-permute-start.2 = (f32[30,62,128]{2,1,0:T(8,128)S(1)}, f32[30,62,128]{2,1,0:T(8,128)S(1)}, u32[]{:S(2)}, u32[]{:S(2)}) collective-permute-start(f32[30,62,128]{2,1,0:T(8,128)S(1)} %copy.121), channel_id=1, source_target_pairs={{0,8},{8,16},{16,24},{24,32},{32,40},{40,48},{48,56},{56,64},{64,7... | collective-permute-start | bytes 2856968 | tf_op jit(solution)/shard_map/ppermute | solution.py:18
  139.2 8.2 %collective-permute-done.4 = f32[48,15,128]{2,1,0:T(8,128)S(1)} collective-permute-done((f32[48,15,128]{2,1,0:T(8,128)S(1)}, f32[48,15,128]{2,1,0:T(8,128)S(1)}, u32[]{:S(2)}, u32[]{:S(2)}) %collective-permute-start.4) | collective-permute-done | bytes 368672 | tf_op jit(solution)/shard_map/ppermute | solution.py:18
  152.3 8.7 %reduce = f32[8,73728]{1,0:T(8,128)} reduce(f32[8,1,73728]{2,1,0:T(1,128)S(1)} %all-to-all-done, f32[]{:T(128)} %broadcast.179), dimensions={1}, to_apply=%all_to_all.13.reduce_sub_computation | reduce | bytes 4718596 | tf_op jit(solution)/shard_map/all_to_all | solution.py:77
  161.1 6.8 %reshape.155 = f32[256,3,16,48]{3,2,1,0:T(8,128)} reshape(f32[8,73728]{1,0:T(8,128)} %reduce) | data formatting | bytes 4718592
  167.9 8.1 %copy.136 = f32[3,48,8,16,32]{1,4,3,2,0:T(8,128)} copy(f32[3,48,8,16,32]{1,3,0,4,2:T(8,128)} %bitcast.334) | data formatting | bytes 4718592 | tf_op jit(solution)/shard_map/all_to_all | solution.py:77
  175.9 5.9 %copy.137 = f32[3,48,128,32]{2,3,1,0:T(8,128)S(1)} copy(f32[3,48,128,32]{1,3,2,0:T(8,128)} %bitcast.335) | data formatting | bytes 4718592 | tf_op jit(solution)/shard_map/all_to_all | solution.py:77
  185.9 6.2 %collective-permute-start.24 = (f32[48,15,128]{2,1,0:T(8,128)S(1)}, f32[48,15,128]{2,1,0:T(8,128)S(1)}, u32[]{:S(2)}, u32[]{:S(2)}) collective-permute-start(f32[48,15,128]{2,1,0:T(8,128)S(1)} %get-tuple-element.81), channel_id=1, source_target_pairs={{0,1},{1,2},{2,3},{3,4},{4,5},{5,6},{6,7},{8,9},{9,10},{10,11},{11... | collective-permute-start | bytes 1105928 | tf_op jit(solution)/shard_map/ppermute | solution.py:18
  221.0 7.3 %collective-permute-start.10 = (f32[30,62,128]{2,1,0:T(8,128)S(1)}, f32[30,62,128]{2,1,0:T(8,128)S(1)}, u32[]{:S(2)}, u32[]{:S(2)}) collective-permute-start(f32[30,62,128]{2,1,0:T(8,128)S(1)} %copy-done.19), channel_id=1, source_target_pairs={{0,8},{8,16},{16,24},{24,32},{32,40},{40,48},{48,56},{56,64},{64,7... | collective-permute-start | bytes 2856968 | tf_op jit(solution)/shard_map/ppermute | solution.py:18
  231.1 7.4 %collective-permute-start.6 = (f32[30,62,128]{2,1,0:T(8,128)S(1)}, f32[30,62,128]{2,1,0:T(8,128)S(1)}, u32[]{:S(2)}, u32[]{:S(2)}) collective-permute-start(f32[30,62,128]{2,1,0:T(8,128)S(1)} %get-tuple-element.43), channel_id=1, source_target_pairs={{0,8},{8,16},{16,24},{24,32},{32,40},{40,48},{48,56},{56,64},{64,7... | collective-permute-start | bytes 2856968 | tf_op jit(solution)/shard_map/ppermute | solution.py:18
  247.0 7.3 %collective-permute-start.26 = (f32[30,62,128]{2,1,0:T(8,128)S(1)}, f32[30,62,128]{2,1,0:T(8,128)S(1)}, u32[]{:S(2)}, u32[]{:S(2)}) collective-permute-start(f32[30,62,128]{2,1,0:T(8,128)S(1)} %get-tuple-element.53), channel_id=1, source_target_pairs={{0,8},{8,16},{16,24},{24,32},{32,40},{40,48},{48,56},{56,64},{64,7... | collective-permute-start | bytes 2856968 | tf_op jit(solution)/shard_map/ppermute | solution.py:18
  264.4 7.3 %collective-permute-start.22 = (f32[30,62,128]{2,1,0:T(8,128)S(1)}, f32[30,62,128]{2,1,0:T(8,128)S(1)}, u32[]{:S(2)}, u32[]{:S(2)}) collective-permute-start(f32[30,62,128]{2,1,0:T(8,128)S(1)} %get-tuple-element.51), channel_id=1, source_target_pairs={{0,8},{8,16},{16,24},{24,32},{32,40},{40,48},{48,56},{56,64},{64,7... | collective-permute-start | bytes 2856968 | tf_op jit(solution)/shard_map/ppermute | solution.py:18
  281.6 7.5 %collective-permute-start.18 = (f32[30,62,128]{2,1,0:T(8,128)S(1)}, f32[30,62,128]{2,1,0:T(8,128)S(1)}, u32[]{:S(2)}, u32[]{:S(2)}) collective-permute-start(f32[30,62,128]{2,1,0:T(8,128)S(1)} %get-tuple-element.49), channel_id=1, source_target_pairs={{0,8},{8,16},{16,24},{24,32},{32,40},{40,48},{48,56},{56,64},{64,7... | collective-permute-start | bytes 2856968 | tf_op jit(solution)/shard_map/ppermute | solution.py:18
  328.7 7.4 %collective-permute-start.30 = (f32[30,62,128]{2,1,0:T(8,128)S(1)}, f32[30,62,128]{2,1,0:T(8,128)S(1)}, u32[]{:S(2)}, u32[]{:S(2)}) collective-permute-start(f32[30,62,128]{2,1,0:T(8,128)S(1)} %get-tuple-element.41), channel_id=1, source_target_pairs={{0,8},{8,16},{16,24},{24,32},{32,40},{40,48},{48,56},{56,64},{64,7... | collective-permute-start | bytes 2856968 | tf_op jit(solution)/shard_map/ppermute | solution.py:18
  336.1 9.7 %collective-permute-done.31 = f32[30,62,128]{2,1,0:T(8,128)S(1)} collective-permute-done((f32[30,62,128]{2,1,0:T(8,128)S(1)}, f32[30,62,128]{2,1,0:T(8,128)S(1)}, u32[]{:S(2)}, u32[]{:S(2)}) %collective-permute-start.31) | collective-permute-done | bytes 952352 | tf_op jit(solution)/shard_map/ppermute | solution.py:20
  376.7 5.9 %collective-permute-start.52 = (f32[48,15,128]{2,1,0:T(8,128)S(1)}, f32[48,15,128]{2,1,0:T(8,128)S(1)}, u32[]{:S(2)}, u32[]{:S(2)}) collective-permute-start(f32[48,15,128]{2,1,0:T(8,128)S(1)} %get-tuple-element.67), channel_id=1, source_target_pairs={{0,1},{1,2},{2,3},{3,4},{4,5},{5,6},{6,7},{8,9},{9,10},{10,11},{11... | collective-permute-start | bytes 1105928 | tf_op jit(solution)/shard_map/ppermute | solution.py:18
  435.4 11.7 %collective-permute-start.54 = (f32[30,62,128]{2,1,0:T(8,128)S(1)}, f32[30,62,128]{2,1,0:T(8,128)S(1)}, u32[]{:S(2)}, u32[]{:S(2)}) collective-permute-start(f32[30,62,128]{2,1,0:T(8,128)S(1)} %get-tuple-element.39), channel_id=1, source_target_pairs={{0,8},{8,16},{16,24},{24,32},{32,40},{40,48},{48,56},{56,64},{64,7... | collective-permute-start | bytes 2856968 | tf_op jit(solution)/shard_map/ppermute | solution.py:18
  449.5 7.3 %collective-permute-start.50 = (f32[30,62,128]{2,1,0:T(8,128)S(1)}, f32[30,62,128]{2,1,0:T(8,128)S(1)}, u32[]{:S(2)}, u32[]{:S(2)}) collective-permute-start(f32[30,62,128]{2,1,0:T(8,128)S(1)} %get-tuple-element.37), channel_id=1, source_target_pairs={{0,8},{8,16},{16,24},{24,32},{32,40},{40,48},{48,56},{56,64},{64,7... | collective-permute-start | bytes 2856968 | tf_op jit(solution)/shard_map/ppermute | solution.py:18
  459.5 7.3 %collective-permute-start.46 = (f32[30,62,128]{2,1,0:T(8,128)S(1)}, f32[30,62,128]{2,1,0:T(8,128)S(1)}, u32[]{:S(2)}, u32[]{:S(2)}) collective-permute-start(f32[30,62,128]{2,1,0:T(8,128)S(1)} %get-tuple-element.35), channel_id=1, source_target_pairs={{0,8},{8,16},{16,24},{24,32},{32,40},{40,48},{48,56},{56,64},{64,7... | collective-permute-start | bytes 2856968 | tf_op jit(solution)/shard_map/ppermute | solution.py:18
  477.3 7.3 %collective-permute-start.42 = (f32[30,62,128]{2,1,0:T(8,128)S(1)}, f32[30,62,128]{2,1,0:T(8,128)S(1)}, u32[]{:S(2)}, u32[]{:S(2)}) collective-permute-start(f32[30,62,128]{2,1,0:T(8,128)S(1)} %get-tuple-element.33), channel_id=1, source_target_pairs={{0,8},{8,16},{16,24},{24,32},{32,40},{40,48},{48,56},{56,64},{64,7... | collective-permute-start | bytes 2856968 | tf_op jit(solution)/shard_map/ppermute | solution.py:18
  494.4 7.3 %collective-permute-start.38 = (f32[30,62,128]{2,1,0:T(8,128)S(1)}, f32[30,62,128]{2,1,0:T(8,128)S(1)}, u32[]{:S(2)}, u32[]{:S(2)}) collective-permute-start(f32[30,62,128]{2,1,0:T(8,128)S(1)} %get-tuple-element.31), channel_id=1, source_target_pairs={{0,8},{8,16},{16,24},{24,32},{32,40},{40,48},{48,56},{56,64},{64,7... | collective-permute-start | bytes 2856968 | tf_op jit(solution)/shard_map/ppermute | solution.py:18
  511.6 7.4 %collective-permute-start.34 = (f32[30,62,128]{2,1,0:T(8,128)S(1)}, f32[30,62,128]{2,1,0:T(8,128)S(1)}, u32[]{:S(2)}, u32[]{:S(2)}) collective-permute-start(f32[30,62,128]{2,1,0:T(8,128)S(1)} %get-tuple-element.29), channel_id=1, source_target_pairs={{0,8},{8,16},{16,24},{24,32},{32,40},{40,48},{48,56},{56,64},{64,7... | collective-permute-start | bytes 2856968 | tf_op jit(solution)/shard_map/ppermute | solution.py:18
  (510 shorter events, 361.5 us)
Async XLA Ops:
  2.2 59.6 %collective-permute-start = (f32[48,15,128]{2,0,1:T(8,128)}, f32[48,15,128]{2,0,1:T(8,128)}, u32[]{:S(2)}, u32[]{:S(2)}) collective-permute-start(f32[48,15,128]{2,0,1:T(8,128)} %copy.306), channel_id=1, source_target_pairs={{0,1},{1,2},{2,3},{3,4},{4,5},{5,6},{6,7},{8,9},{9,10},{10,11},{11... | collective-permute-start | bytes 1105928 | tf_op jit(solution)/shard_map/ppermute | solution.py:18
  5.5 57.8 %collective-permute-start.1 = (f32[48,15,128]{2,0,1:T(8,128)S(1)}, f32[48,15,128]{2,0,1:T(8,128)}, u32[]{:S(2)}, u32[]{:S(2)}) collective-permute-start(f32[48,15,128]{2,0,1:T(8,128)S(1)} %copy.307), channel_id=1, source_target_pairs={{1,0},{2,1},{3,2},{4,3},{5,4},{6,5},{7,6},{9,8},{10,9},{11,10},{12... | collective-permute-start | bytes 1105928 | tf_op jit(solution)/shard_map/ppermute | solution.py:20
  22.6 129.2 %all-to-all-start = ((f32[8,1,73728]{2,1,0:T(1,128)}), f32[8,1,73728]{2,1,0:T(1,128)S(1)}, u32[]{:S(2)}, u32[]{:S(2)}) async-start(f32[8,1,73728]{2,1,0:T(1,128)} %reshape.154), calls=%async_computation | async-start | bytes 4718592 | tf_op jit(solution)/shard_map/all_to_all | solution.py:77
  94.0 36.3 %collective-permute-start.13 = (f32[48,15,128]{2,1,0:T(8,128)S(1)}, f32[48,15,128]{2,1,0:T(8,128)S(1)}, u32[]{:S(2)}, u32[]{:S(2)}) collective-permute-start(f32[48,15,128]{2,1,0:T(8,128)S(1)} %get-tuple-element.76), channel_id=1, source_target_pairs={{1,0},{2,1},{3,2},{4,3},{5,4},{6,5},{7,6},{9,8},{10,9},{11,10},{12... | collective-permute-start | bytes 1105928 | tf_op jit(solution)/shard_map/ppermute | solution.py:20
  96.5 39.8 %collective-permute-start.12 = (f32[48,15,128]{2,1,0:T(8,128)S(1)}, f32[48,15,128]{2,1,0:T(8,128)S(1)}, u32[]{:S(2)}, u32[]{:S(2)}) collective-permute-start(f32[48,15,128]{2,1,0:T(8,128)S(1)} %get-tuple-element.75), channel_id=1, source_target_pairs={{0,1},{1,2},{2,3},{3,4},{4,5},{5,6},{6,7},{8,9},{9,10},{10,11},{11... | collective-permute-start | bytes 1105928 | tf_op jit(solution)/shard_map/ppermute | solution.py:18
  221.0 33.2 %collective-permute-start.10 = (f32[30,62,128]{2,1,0:T(8,128)S(1)}, f32[30,62,128]{2,1,0:T(8,128)S(1)}, u32[]{:S(2)}, u32[]{:S(2)}) collective-permute-start(f32[30,62,128]{2,1,0:T(8,128)S(1)} %copy-done.19), channel_id=1, source_target_pairs={{0,8},{8,16},{16,24},{24,32},{32,40},{40,48},{48,56},{56,64},{64,7... | collective-permute-start | bytes 2856968 | tf_op jit(solution)/shard_map/ppermute | solution.py:18
  228.3 36.1 %collective-permute-start.7 = (f32[30,62,128]{2,1,0:T(8,128)S(1)}, f32[30,62,128]{2,1,0:T(8,128)S(1)}, u32[]{:S(2)}, u32[]{:S(2)}) collective-permute-start(f32[30,62,128]{2,1,0:T(8,128)S(1)} %get-tuple-element.44), channel_id=1, source_target_pairs={{8,0},{16,8},{24,16},{32,24},{40,32},{48,40},{56,48},{64,56},{72,6... | collective-permute-start | bytes 2856968 | tf_op jit(solution)/shard_map/ppermute | solution.py:20
  231.1 40.5 %collective-permute-start.6 = (f32[30,62,128]{2,1,0:T(8,128)S(1)}, f32[30,62,128]{2,1,0:T(8,128)S(1)}, u32[]{:S(2)}, u32[]{:S(2)}) collective-permute-start(f32[30,62,128]{2,1,0:T(8,128)S(1)} %get-tuple-element.43), channel_id=1, source_target_pairs={{0,8},{8,16},{16,24},{24,32},{32,40},{40,48},{48,56},{56,64},{64,7... | collective-permute-start | bytes 2856968 | tf_op jit(solution)/shard_map/ppermute | solution.py:18
  238.6 43.0 %collective-permute-start.27 = (f32[30,62,128]{2,1,0:T(8,128)S(1)}, f32[30,62,128]{2,1,0:T(8,128)S(1)}, u32[]{:S(2)}, u32[]{:S(2)}) collective-permute-start(f32[30,62,128]{2,1,0:T(8,128)S(1)} %get-tuple-element.54), channel_id=1, source_target_pairs={{8,0},{16,8},{24,16},{32,24},{40,32},{48,40},{56,48},{64,56},{72,6... | collective-permute-start | bytes 2856968 | tf_op jit(solution)/shard_map/ppermute | solution.py:20
  247.0 42.1 %collective-permute-start.26 = (f32[30,62,128]{2,1,0:T(8,128)S(1)}, f32[30,62,128]{2,1,0:T(8,128)S(1)}, u32[]{:S(2)}, u32[]{:S(2)}) collective-permute-start(f32[30,62,128]{2,1,0:T(8,128)S(1)} %get-tuple-element.53), channel_id=1, source_target_pairs={{0,8},{8,16},{16,24},{24,32},{32,40},{40,48},{48,56},{56,64},{64,7... | collective-permute-start | bytes 2856968 | tf_op jit(solution)/shard_map/ppermute | solution.py:18
  254.3 42.5 %collective-permute-start.23 = (f32[30,62,128]{2,1,0:T(8,128)S(1)}, f32[30,62,128]{2,1,0:T(8,128)S(1)}, u32[]{:S(2)}, u32[]{:S(2)}) collective-permute-start(f32[30,62,128]{2,1,0:T(8,128)S(1)} %get-tuple-element.52), channel_id=1, source_target_pairs={{8,0},{16,8},{24,16},{32,24},{40,32},{48,40},{56,48},{64,56},{72,6... | collective-permute-start | bytes 2856968 | tf_op jit(solution)/shard_map/ppermute | solution.py:20
  264.4 32.3 %collective-permute-start.22 = (f32[30,62,128]{2,1,0:T(8,128)S(1)}, f32[30,62,128]{2,1,0:T(8,128)S(1)}, u32[]{:S(2)}, u32[]{:S(2)}) collective-permute-start(f32[30,62,128]{2,1,0:T(8,128)S(1)} %get-tuple-element.51), channel_id=1, source_target_pairs={{0,8},{8,16},{16,24},{24,32},{32,40},{40,48},{48,56},{56,64},{64,7... | collective-permute-start | bytes 2856968 | tf_op jit(solution)/shard_map/ppermute | solution.py:18
  271.7 33.1 %collective-permute-start.19 = (f32[30,62,128]{2,1,0:T(8,128)S(1)}, f32[30,62,128]{2,1,0:T(8,128)S(1)}, u32[]{:S(2)}, u32[]{:S(2)}) collective-permute-start(f32[30,62,128]{2,1,0:T(8,128)S(1)} %get-tuple-element.50), channel_id=1, source_target_pairs={{8,0},{16,8},{24,16},{32,24},{40,32},{48,40},{56,48},{64,56},{72,6... | collective-permute-start | bytes 2856968 | tf_op jit(solution)/shard_map/ppermute | solution.py:20
  376.7 33.2 %collective-permute-start.52 = (f32[48,15,128]{2,1,0:T(8,128)S(1)}, f32[48,15,128]{2,1,0:T(8,128)S(1)}, u32[]{:S(2)}, u32[]{:S(2)}) collective-permute-start(f32[48,15,128]{2,1,0:T(8,128)S(1)} %get-tuple-element.67), channel_id=1, source_target_pairs={{0,1},{1,2},{2,3},{3,4},{4,5},{5,6},{6,7},{8,9},{9,10},{10,11},{11... | collective-permute-start | bytes 1105928 | tf_op jit(solution)/shard_map/ppermute | solution.py:18
  386.9 30.6 %collective-permute-start.48 = (f32[48,15,128]{2,1,0:T(8,128)S(1)}, f32[48,15,128]{2,1,0:T(8,128)S(1)}, u32[]{:S(2)}, u32[]{:S(2)}) collective-permute-start(f32[48,15,128]{2,1,0:T(8,128)S(1)} %get-tuple-element.65), channel_id=1, source_target_pairs={{0,1},{1,2},{2,3},{3,4},{4,5},{5,6},{6,7},{8,9},{9,10},{10,11},{11... | collective-permute-start | bytes 1105928 | tf_op jit(solution)/shard_map/ppermute | solution.py:18
  435.4 31.4 %collective-permute-start.54 = (f32[30,62,128]{2,1,0:T(8,128)S(1)}, f32[30,62,128]{2,1,0:T(8,128)S(1)}, u32[]{:S(2)}, u32[]{:S(2)}) collective-permute-start(f32[30,62,128]{2,1,0:T(8,128)S(1)} %get-tuple-element.39), channel_id=1, source_target_pairs={{0,8},{8,16},{16,24},{24,32},{32,40},{40,48},{48,56},{56,64},{64,7... | collective-permute-start | bytes 2856968 | tf_op jit(solution)/shard_map/ppermute | solution.py:18
  449.5 35.2 %collective-permute-start.50 = (f32[30,62,128]{2,1,0:T(8,128)S(1)}, f32[30,62,128]{2,1,0:T(8,128)S(1)}, u32[]{:S(2)}, u32[]{:S(2)}) collective-permute-start(f32[30,62,128]{2,1,0:T(8,128)S(1)} %get-tuple-element.37), channel_id=1, source_target_pairs={{0,8},{8,16},{16,24},{24,32},{32,40},{40,48},{48,56},{56,64},{64,7... | collective-permute-start | bytes 2856968 | tf_op jit(solution)/shard_map/ppermute | solution.py:18
  456.7 37.6 %collective-permute-start.47 = (f32[30,62,128]{2,1,0:T(8,128)S(1)}, f32[30,62,128]{2,1,0:T(8,128)S(1)}, u32[]{:S(2)}, u32[]{:S(2)}) collective-permute-start(f32[30,62,128]{2,1,0:T(8,128)S(1)} %get-tuple-element.36), channel_id=1, source_target_pairs={{8,0},{16,8},{24,16},{32,24},{40,32},{48,40},{56,48},{64,56},{72,6... | collective-permute-start | bytes 2856968 | tf_op jit(solution)/shard_map/ppermute | solution.py:20
  459.5 42.1 %collective-permute-start.46 = (f32[30,62,128]{2,1,0:T(8,128)S(1)}, f32[30,62,128]{2,1,0:T(8,128)S(1)}, u32[]{:S(2)}, u32[]{:S(2)}) collective-permute-start(f32[30,62,128]{2,1,0:T(8,128)S(1)} %get-tuple-element.35), channel_id=1, source_target_pairs={{0,8},{8,16},{16,24},{24,32},{32,40},{40,48},{48,56},{56,64},{64,7... | collective-permute-start | bytes 2856968 | tf_op jit(solution)/shard_map/ppermute | solution.py:18
  466.8 44.7 %collective-permute-start.43 = (f32[30,62,128]{2,1,0:T(8,128)S(1)}, f32[30,62,128]{2,1,0:T(8,128)S(1)}, u32[]{:S(2)}, u32[]{:S(2)}) collective-permute-start(f32[30,62,128]{2,1,0:T(8,128)S(1)} %get-tuple-element.34), channel_id=1, source_target_pairs={{8,0},{16,8},{24,16},{32,24},{40,32},{48,40},{56,48},{64,56},{72,6... | collective-permute-start | bytes 2856968 | tf_op jit(solution)/shard_map/ppermute | solution.py:20
  477.3 41.7 %collective-permute-start.42 = (f32[30,62,128]{2,1,0:T(8,128)S(1)}, f32[30,62,128]{2,1,0:T(8,128)S(1)}, u32[]{:S(2)}, u32[]{:S(2)}) collective-permute-start(f32[30,62,128]{2,1,0:T(8,128)S(1)} %get-tuple-element.33), channel_id=1, source_target_pairs={{0,8},{8,16},{16,24},{24,32},{32,40},{40,48},{48,56},{56,64},{64,7... | collective-permute-start | bytes 2856968 | tf_op jit(solution)/shard_map/ppermute | solution.py:18
  484.6 42.0 %collective-permute-start.39 = (f32[30,62,128]{2,1,0:T(8,128)S(1)}, f32[30,62,128]{2,1,0:T(8,128)S(1)}, u32[]{:S(2)}, u32[]{:S(2)}) collective-permute-start(f32[30,62,128]{2,1,0:T(8,128)S(1)} %get-tuple-element.32), channel_id=1, source_target_pairs={{8,0},{16,8},{24,16},{32,24},{40,32},{48,40},{56,48},{64,56},{72,6... | collective-permute-start | bytes 2856968 | tf_op jit(solution)/shard_map/ppermute | solution.py:20
  494.4 32.2 %collective-permute-start.38 = (f32[30,62,128]{2,1,0:T(8,128)S(1)}, f32[30,62,128]{2,1,0:T(8,128)S(1)}, u32[]{:S(2)}, u32[]{:S(2)}) collective-permute-start(f32[30,62,128]{2,1,0:T(8,128)S(1)} %get-tuple-element.31), channel_id=1, source_target_pairs={{0,8},{8,16},{16,24},{24,32},{32,40},{40,48},{48,56},{56,64},{64,7... | collective-permute-start | bytes 2856968 | tf_op jit(solution)/shard_map/ppermute | solution.py:18
  501.7 32.9 %collective-permute-start.35 = (f32[30,62,128]{2,1,0:T(8,128)S(1)}, f32[30,62,128]{2,1,0:T(8,128)S(1)}, u32[]{:S(2)}, u32[]{:S(2)}) collective-permute-start(f32[30,62,128]{2,1,0:T(8,128)S(1)} %get-tuple-element.30), channel_id=1, source_target_pairs={{8,0},{16,8},{24,16},{32,24},{40,32},{48,40},{56,48},{64,56},{72,6... | collective-permute-start | bytes 2856968 | tf_op jit(solution)/shard_map/ppermute | solution.py:20
  (153 other events, 2298.4 us)
where the time goes:
time: 552 us; the launch traced here: 544 us
  starting transfers between devices  244 us (44%)
  matrix products  156 us (28%)
  local copies, waits for them, and re-layouts  68.4 us (12%)
  other arithmetic  41.3 us (7%)
  waiting for transfers between devices  30.5 us (6%)
    ppermute x28, starting transfers between devices, padded(): lax.ppermute(tail, axis, [(i, (i + 1) % count) for i in range(ends)])  176 us
    ppermute x28, starting transfers between devices, padded(): lax.ppermute(head, axis, [((i + 1) % count, i) for i in range(ends)])  61.3 us
    dot_general x12, matrix products, local(): jnp.einsum('zj,jyx->zyx', adjoint_depth[number], rimmed, precision=exact_...  48.6 us
    dot_general x12, matrix products, blur_forward(): jnp.einsum('zj,jyx->zyx', band_depth, haloed, precision=exact_mode)  37.9 us
    unnamed x247, local copies, waits for them, and re-layouts  25.3 us
    dot_general x12, matrix products, blur_forward(): jnp.einsum('yj,zjx->zyx', band_rows, section, precision=exact_mode)  21.3 us
    dot_general x12, matrix products, local(): jnp.einsum('yj,zjx->zyx', adjoint_rows[number], back, precision=exact_mode)  18.9 us
    dot_general x12, matrix products, local(): jnp.einsum('zyj,jx->zyx', back, laterals[number], precision=exact_mode)  18.1 us
  transfers between devices with their start and end apart: 57, of which 8 were waited for; matrix products, arithmetic and copies ran while one was open for 34% of the time, Pallas kernels for 0%

commit v1 on v0

--- a/solution.py
+++ b/solution.py
@@ -74,7 +74,13 @@
     reach_depth = (kernel_depth.shape[1] - 1) // 2
     reach_rows = (kernel_rows.shape[1] - 1) // 2
     turned = jnp.transpose(
-        lax.all_to_all(views_turned, "xy", split_axis=3, concat_axis=2, tiled=True), (0, 1, 3, 2)
+        jnp.concatenate(
+            lax.all_to_all(
+                jnp.stack(jnp.split(views_turned, lax.axis_size("xy"), axis=3)), "xy", 0, 0
+            ),
+            axis=2,
+        ),
+        (0, 1, 3, 2),
     )
     observed = jnp.concatenate([views_upright, turned], axis=0)
     taps_depth = normalize(kernel_depth)

time: 552 us -> 559 us (1.013)
  the two profiles are of different devices: /device:TPU:31 before, /device:TPU:104 now
where the time goes in v1:
time: 559 us; the launch traced here: 548 us
  starting transfers between devices  217 us (39%)
  matrix products  156 us (28%)
  local copies, waits for them, and re-layouts  79.5 us (14%)
  waiting for transfers between devices  59.6 us (11%)
  other arithmetic  33.1 us (6%)
    ppermute x28, starting transfers between devices, padded(): lax.ppermute(head, axis, [((i + 1) % count, i) for i in range(ends)])  147 us
    ppermute x28, starting transfers between devices, padded(): lax.ppermute(tail, axis, [(i, (i + 1) % count) for i in range(ends)])  63.5 us
    dot_general x12, matrix products, local(): jnp.einsum('zj,jyx->zyx', adjoint_depth[number], rimmed, precision=exact_...  48.7 us
    ppermute x28, waiting for transfers between devices, padded(): lax.ppermute(tail, axis, [(i, (i + 1) % count) for i in range(ends)])  45.3 us
    unnamed x243, local copies, waits for them, and re-layouts  42.7 us
    dot_general x12, matrix products, blur_forward(): jnp.einsum('zj,jyx->zyx', band_depth, haloed, precision=exact_mode)  37.8 us
    dot_general x12, matrix products, blur_forward(): jnp.einsum('yj,zjx->zyx', band_rows, section, precision=exact_mode)  21.3 us
    dot_general x12, matrix products, local(): jnp.einsum('yj,zjx->zyx', adjoint_rows[number], back, precision=exact_mode)  18.9 us
  transfers between devices with their start and end apart: 57, of which 12 were waited for; matrix products, arithmetic and copies ran while one was open for 33% of the time, Pallas kernels for 0%

profile of v1, /device:TPU:104, one launch (start us, length us, event | category | flops | bytes accessed | tf_op | source)
XLA Modules:
  0.0 547.9 jit_solution(10288373198801928763)
XLA Ops:
  36.4 9.5 %reshape.162 = f32[8,1,73728]{2,1,0:T(1,128)} reshape(f32[8,3,16,32,48]{4,3,2,1,0:T(8,128)} %bitcast.321) | data formatting | bytes 4718592
  45.9 6.5 %all-to-all-start = ((f32[8,1,73728]{2,1,0:T(1,128)}), f32[8,1,73728]{2,1,0:T(1,128)S(1)}, u32[]{:S(2)}, u32[]{:S(2)}) async-start(f32[8,1,73728]{2,1,0:T(1,128)} %reshape.162), calls=%async_computation | async-start | bytes 4718592 | tf_op jit(solution)/shard_map/all_to_all | solution.py:78
  80.7 8.0 %collective-permute-done.3 = f32[30,62,128]{2,1,0:T(8,128)S(1)} collective-permute-done((f32[30,62,128]{2,1,0:T(8,128)S(1)}, f32[30,62,128]{2,1,0:T(8,128)S(1)}, u32[]{:S(2)}, u32[]{:S(2)}) %collective-permute-start.3) | collective-permute-done | bytes 952352 | tf_op jit(solution)/shard_map/ppermute | solution.py:20
  149.1 8.7 %reduce = f32[8,73728]{1,0:T(8,128)} reduce(f32[8,1,73728]{2,1,0:T(1,128)S(1)} %all-to-all-done, f32[]{:T(128)} %broadcast.179), dimensions={1}, to_apply=%all_to_all.3.reduce_sub_computation | reduce | bytes 4718596 | tf_op jit(solution)/shard_map/all_to_all | solution.py:78
  157.8 6.8 %reshape.163 = f32[8,3,16,32,48]{4,3,2,1,0:T(8,128)} reshape(f32[8,73728]{1,0:T(8,128)} %reduce) | data formatting | bytes 4718592
  171.6 5.9 %copy.155 = f32[3,48,128,32]{2,3,1,0:T(8,128)S(1)} copy(f32[3,48,128,32]{1,3,2,0:T(8,128)} %bitcast.349) | data formatting | bytes 4718592 | tf_op jit(solution)/shard_map/reshape | solution.py:77
  188.7 6.0 %collective-permute-start.25 = (f32[48,15,128]{2,1,0:T(8,128)S(1)}, f32[48,15,128]{2,1,0:T(8,128)S(1)}, u32[]{:S(2)}, u32[]{:S(2)}) collective-permute-start(f32[48,15,128]{2,1,0:T(8,128)S(1)} %get-tuple-element.90), channel_id=1, source_target_pairs={{1,0},{2,1},{3,2},{4,3},{5,4},{6,5},{7,6},{9,8},{10,9},{11,10},{12... | collective-permute-start | bytes 1105928 | tf_op jit(solution)/shard_map/ppermute | solution.py:20
  202.2 5.7 %collective-permute-start.21 = (f32[48,15,128]{2,1,0:T(8,128)S(1)}, f32[48,15,128]{2,1,0:T(8,128)S(1)}, u32[]{:S(2)}, u32[]{:S(2)}) collective-permute-start(f32[48,15,128]{2,1,0:T(8,128)S(1)} %get-tuple-element.88), channel_id=1, source_target_pairs={{1,0},{2,1},{3,2},{4,3},{5,4},{6,5},{7,6},{9,8},{10,9},{11,10},{12... | collective-permute-start | bytes 1105928 | tf_op jit(solution)/shard_map/ppermute | solution.py:20
  213.8 7.3 %collective-permute-start.15 = (f32[30,62,128]{2,1,0:T(8,128)S(1)}, f32[30,62,128]{2,1,0:T(8,128)S(1)}, u32[]{:S(2)}, u32[]{:S(2)}) collective-permute-start(f32[30,62,128]{2,1,0:T(8,128)S(1)} %copy-done.27), channel_id=1, source_target_pairs={{8,0},{16,8},{24,16},{32,24},{40,32},{48,40},{56,48},{64,56},{72,6... | collective-permute-start | bytes 2856968 | tf_op jit(solution)/shard_map/ppermute | solution.py:20
  223.2 7.3 %collective-permute-start.11 = (f32[30,62,128]{2,1,0:T(8,128)}, f32[30,62,128]{2,1,0:T(8,128)S(1)}, u32[]{:S(2)}, u32[]{:S(2)}) collective-permute-start(f32[30,62,128]{2,1,0:T(8,128)} %get-tuple-element.54), channel_id=1, source_target_pairs={{8,0},{16,8},{24,16},{32,24},{40,32},{48,40},{56,48},{64,56},{72,6... | collective-permute-start | bytes 2856968 | tf_op jit(solution)/shard_map/ppermute | solution.py:20
  231.4 7.9 %collective-permute-done.14 = f32[30,62,128]{2,1,0:T(8,128)S(1)} collective-permute-done((f32[30,62,128]{2,1,0:T(8,128)S(1)}, f32[30,62,128]{2,1,0:T(8,128)S(1)}, u32[]{:S(2)}, u32[]{:S(2)}) %collective-permute-start.14) | collective-permute-done | bytes 952352 | tf_op jit(solution)/shard_map/ppermute | solution.py:18
  250.1 6.8 %collective-permute-start.27 = (f32[30,62,128]{2,1,0:T(8,128)S(1)}, f32[30,62,128]{2,1,0:T(8,128)S(1)}, u32[]{:S(2)}, u32[]{:S(2)}) collective-permute-start(f32[30,62,128]{2,1,0:T(8,128)S(1)} %get-tuple-element.62), channel_id=1, source_target_pairs={{8,0},{16,8},{24,16},{32,24},{40,32},{48,40},{56,48},{64,56},{72,6... | collective-permute-start | bytes 2856968 | tf_op jit(solution)/shard_map/ppermute | solution.py:20
  267.0 7.3 %collective-permute-start.23 = (f32[30,62,128]{2,1,0:T(8,128)S(1)}, f32[30,62,128]{2,1,0:T(8,128)S(1)}, u32[]{:S(2)}, u32[]{:S(2)}) collective-permute-start(f32[30,62,128]{2,1,0:T(8,128)S(1)} %get-tuple-element.60), channel_id=1, source_target_pairs={{8,0},{16,8},{24,16},{32,24},{40,32},{48,40},{56,48},{64,56},{72,6... | collective-permute-start | bytes 2856968 | tf_op jit(solution)/shard_map/ppermute | solution.py:20
  284.2 7.5 %collective-permute-start.19 = (f32[30,62,128]{2,1,0:T(8,128)S(1)}, f32[30,62,128]{2,1,0:T(8,128)S(1)}, u32[]{:S(2)}, u32[]{:S(2)}) collective-permute-start(f32[30,62,128]{2,1,0:T(8,128)S(1)} %get-tuple-element.58), channel_id=1, source_target_pairs={{8,0},{16,8},{24,16},{32,24},{40,32},{48,40},{56,48},{64,56},{72,6... | collective-permute-start | bytes 2856968 | tf_op jit(solution)/shard_map/ppermute | solution.py:20
  330.6 7.4 %collective-permute-start.31 = (f32[30,62,128]{2,1,0:T(8,128)S(1)}, f32[30,62,128]{2,1,0:T(8,128)S(1)}, u32[]{:S(2)}, u32[]{:S(2)}) collective-permute-start(f32[30,62,128]{2,1,0:T(8,128)S(1)} %get-tuple-element.50), channel_id=1, source_target_pairs={{8,0},{16,8},{24,16},{32,24},{40,32},{48,40},{56,48},{64,56},{72,6... | collective-permute-start | bytes 2856968 | tf_op jit(solution)/shard_map/ppermute | solution.py:20
  338.0 9.7 %collective-permute-done.30 = f32[30,62,128]{2,1,0:T(8,128)S(1)} collective-permute-done((f32[30,62,128]{2,1,0:T(8,128)S(1)}, f32[30,62,128]{2,1,0:T(8,128)S(1)}, u32[]{:S(2)}, u32[]{:S(2)}) %collective-permute-start.30) | collective-permute-done | bytes 952352 | tf_op jit(solution)/shard_map/ppermute | solution.py:18
  397.2 6.1 %collective-permute-start.53 = (f32[48,15,128]{2,1,0:T(8,128)S(1)}, f32[48,15,128]{2,1,0:T(8,128)S(1)}, u32[]{:S(2)}, u32[]{:S(2)}) collective-permute-start(f32[48,15,128]{2,1,0:T(8,128)S(1)} %get-tuple-element.76), channel_id=1, source_target_pairs={{1,0},{2,1},{3,2},{4,3},{5,4},{6,5},{7,6},{9,8},{10,9},{11,10},{12... | collective-permute-start | bytes 1105928 | tf_op jit(solution)/shard_map/ppermute | solution.py:20
  408.5 6.7 %collective-permute-start.33 = (f32[48,15,128]{2,1,0:T(8,128)S(1)}, f32[48,15,128]{2,1,0:T(8,128)S(1)}, u32[]{:S(2)}, u32[]{:S(2)}) collective-permute-start(f32[48,15,128]{2,1,0:T(8,128)S(1)} %get-tuple-element.66), channel_id=1, source_target_pairs={{1,0},{2,1},{3,2},{4,3},{5,4},{6,5},{7,6},{9,8},{10,9},{11,10},{12... | collective-permute-start | bytes 1105928 | tf_op jit(solution)/shard_map/ppermute | solution.py:20
  431.1 8.1 %collective-permute-done.44 = f32[48,15,128]{2,1,0:T(8,128)S(1)} collective-permute-done((f32[48,15,128]{2,1,0:T(8,128)S(1)}, f32[48,15,128]{2,1,0:T(8,128)S(1)}, u32[]{:S(2)}, u32[]{:S(2)}) %collective-permute-start.44) | collective-permute-done | bytes 368672 | tf_op jit(solution)/shard_map/ppermute | solution.py:18
  447.3 7.3 %collective-permute-start.55 = (f32[30,62,128]{2,1,0:T(8,128)S(1)}, f32[30,62,128]{2,1,0:T(8,128)S(1)}, u32[]{:S(2)}, u32[]{:S(2)}) collective-permute-start(f32[30,62,128]{2,1,0:T(8,128)S(1)} %get-tuple-element.48), channel_id=1, source_target_pairs={{8,0},{16,8},{24,16},{32,24},{40,32},{48,40},{56,48},{64,56},{72,6... | collective-permute-start | bytes 2856968 | tf_op jit(solution)/shard_map/ppermute | solution.py:20
  458.9 7.3 %collective-permute-start.51 = (f32[30,62,128]{2,1,0:T(8,128)S(1)}, f32[30,62,128]{2,1,0:T(8,128)S(1)}, u32[]{:S(2)}, u32[]{:S(2)}) collective-permute-start(f32[30,62,128]{2,1,0:T(8,128)S(1)} %get-tuple-element.46), channel_id=1, source_target_pairs={{8,0},{16,8},{24,16},{32,24},{40,32},{48,40},{56,48},{64,56},{72,6... | collective-permute-start | bytes 2856968 | tf_op jit(solution)/shard_map/ppermute | solution.py:20
  478.5 6.5 %collective-permute-done.50 = f32[30,62,128]{2,1,0:T(8,128)S(1)} collective-permute-done((f32[30,62,128]{2,1,0:T(8,128)S(1)}, f32[30,62,128]{2,1,0:T(8,128)S(1)}, u32[]{:S(2)}, u32[]{:S(2)}) %collective-permute-start.50) | collective-permute-done | bytes 952352 | tf_op jit(solution)/shard_map/ppermute | solution.py:18
  497.4 6.8 %collective-permute-start.43 = (f32[30,62,128]{2,1,0:T(8,128)S(1)}, f32[30,62,128]{2,1,0:T(8,128)S(1)}, u32[]{:S(2)}, u32[]{:S(2)}) collective-permute-start(f32[30,62,128]{2,1,0:T(8,128)S(1)} %get-tuple-element.42), channel_id=1, source_target_pairs={{8,0},{16,8},{24,16},{32,24},{40,32},{48,40},{56,48},{64,56},{72,6... | collective-permute-start | bytes 2856968 | tf_op jit(solution)/shard_map/ppermute | solution.py:20
  514.3 7.6 %collective-permute-start.39 = (f32[30,62,128]{2,1,0:T(8,128)S(1)}, f32[30,62,128]{2,1,0:T(8,128)S(1)}, u32[]{:S(2)}, u32[]{:S(2)}) collective-permute-start(f32[30,62,128]{2,1,0:T(8,128)S(1)} %get-tuple-element.40), channel_id=1, source_target_pairs={{8,0},{16,8},{24,16},{32,24},{40,32},{48,40},{56,48},{64,56},{72,6... | collective-permute-start | bytes 2856968 | tf_op jit(solution)/shard_map/ppermute | solution.py:20
  (509 shorter events, 370.0 us)
Async XLA Ops:
  2.2 62.7 %collective-permute-start = (f32[48,15,128]{2,0,1:T(8,128)}, f32[48,15,128]{2,0,1:T(8,128)}, u32[]{:S(2)}, u32[]{:S(2)}) collective-permute-start(f32[48,15,128]{2,0,1:T(8,128)} %copy.330), channel_id=1, source_target_pairs={{0,1},{1,2},{2,3},{3,4},{4,5},{5,6},{6,7},{8,9},{9,10},{10,11},{11... | collective-permute-start | bytes 1105928 | tf_op jit(solution)/shard_map/ppermute | solution.py:18
  6.5 59.8 %collective-permute-start.1 = (f32[48,15,128]{2,0,1:T(8,128)}, f32[48,15,128]{2,0,1:T(8,128)}, u32[]{:S(2)}, u32[]{:S(2)}) collective-permute-start(f32[48,15,128]{2,0,1:T(8,128)} %copy.331), channel_id=1, source_target_pairs={{1,0},{2,1},{3,2},{4,3},{5,4},{6,5},{7,6},{9,8},{10,9},{11,10},{12... | collective-permute-start | bytes 1105928 | tf_op jit(solution)/shard_map/ppermute | solution.py:20
  45.9 102.7 %all-to-all-start = ((f32[8,1,73728]{2,1,0:T(1,128)}), f32[8,1,73728]{2,1,0:T(1,128)S(1)}, u32[]{:S(2)}, u32[]{:S(2)}) async-start(f32[8,1,73728]{2,1,0:T(1,128)} %reshape.162), calls=%async_computation | async-start | bytes 4718592 | tf_op jit(solution)/shard_map/all_to_all | solution.py:78
  96.4 47.7 %collective-permute-start.8 = (f32[48,15,128]{2,1,0:T(8,128)S(1)}, f32[48,15,128]{2,1,0:T(8,128)S(1)}, u32[]{:S(2)}, u32[]{:S(2)}) collective-permute-start(f32[48,15,128]{2,1,0:T(8,128)S(1)} %get-tuple-element.81), channel_id=1, source_target_pairs={{0,1},{1,2},{2,3},{3,4},{4,5},{5,6},{6,7},{8,9},{9,10},{10,11},{11... | collective-permute-start | bytes 1105928 | tf_op jit(solution)/shard_map/ppermute | solution.py:18
  99.8 44.3 %collective-permute-start.9 = (f32[48,15,128]{2,1,0:T(8,128)S(1)}, f32[48,15,128]{2,1,0:T(8,128)S(1)}, u32[]{:S(2)}, u32[]{:S(2)}) collective-permute-start(f32[48,15,128]{2,1,0:T(8,128)S(1)} %get-tuple-element.82), channel_id=1, source_target_pairs={{1,0},{2,1},{3,2},{4,3},{5,4},{6,5},{7,6},{9,8},{10,9},{11,10},{12... | collective-permute-start | bytes 1105928 | tf_op jit(solution)/shard_map/ppermute | solution.py:20
  107.2 34.2 %collective-permute-start.12 = (f32[48,15,128]{2,1,0:T(8,128)S(1)}, f32[48,15,128]{2,1,0:T(8,128)S(1)}, u32[]{:S(2)}, u32[]{:S(2)}) collective-permute-start(f32[48,15,128]{2,1,0:T(8,128)S(1)} %get-tuple-element.83), channel_id=1, source_target_pairs={{0,1},{1,2},{2,3},{3,4},{4,5},{5,6},{6,7},{8,9},{9,10},{10,11},{11... | collective-permute-start | bytes 1105928 | tf_op jit(solution)/shard_map/ppermute | solution.py:18
  179.6 41.7 %collective-permute-start.16 = (f32[48,15,128]{2,1,0:T(8,128)S(1)}, f32[48,15,128]{2,1,0:T(8,128)S(1)}, u32[]{:S(2)}, u32[]{:S(2)}) collective-permute-start(f32[48,15,128]{2,1,0:T(8,128)S(1)} %get-tuple-element.85), channel_id=1, source_target_pairs={{0,1},{1,2},{2,3},{3,4},{4,5},{5,6},{6,7},{8,9},{9,10},{10,11},{11... | collective-permute-start | bytes 1105928 | tf_op jit(solution)/shard_map/ppermute | solution.py:18
  181.8 41.4 %collective-permute-start.17 = (f32[48,15,128]{2,1,0:T(8,128)S(1)}, f32[48,15,128]{2,1,0:T(8,128)S(1)}, u32[]{:S(2)}, u32[]{:S(2)}) collective-permute-start(f32[48,15,128]{2,1,0:T(8,128)S(1)} %get-tuple-element.86), channel_id=1, source_target_pairs={{1,0},{2,1},{3,2},{4,3},{5,4},{6,5},{7,6},{9,8},{10,9},{11,10},{12... | collective-permute-start | bytes 1105928 | tf_op jit(solution)/shard_map/ppermute | solution.py:20
  209.5 57.5 %collective-permute-start.6 = (f32[30,62,128]{2,1,0:T(8,128)S(1)}, f32[30,62,128]{2,1,0:T(8,128)S(1)}, u32[]{:S(2)}, u32[]{:S(2)}) collective-permute-start(f32[30,62,128]{2,1,0:T(8,128)S(1)} %copy-done.26), channel_id=1, source_target_pairs={{0,8},{8,16},{16,24},{24,32},{32,40},{40,48},{48,56},{56,64},{64,7... | collective-permute-start | bytes 2856968 | tf_op jit(solution)/shard_map/ppermute | solution.py:18
  221.3 28.8 %collective-permute-start.10 = (f32[30,62,128]{2,1,0:T(8,128)}, f32[30,62,128]{2,1,0:T(8,128)S(1)}, u32[]{:S(2)}, u32[]{:S(2)}) collective-permute-start(f32[30,62,128]{2,1,0:T(8,128)} %get-tuple-element.53), channel_id=1, source_target_pairs={{0,8},{8,16},{16,24},{24,32},{32,40},{40,48},{48,56},{56,64},{64,7... | collective-permute-start | bytes 2856968 | tf_op jit(solution)/shard_map/ppermute | solution.py:18
  223.2 33.6 %collective-permute-start.11 = (f32[30,62,128]{2,1,0:T(8,128)}, f32[30,62,128]{2,1,0:T(8,128)S(1)}, u32[]{:S(2)}, u32[]{:S(2)}) collective-permute-start(f32[30,62,128]{2,1,0:T(8,128)} %get-tuple-element.54), channel_id=1, source_target_pairs={{8,0},{16,8},{24,16},{32,24},{40,32},{48,40},{56,48},{64,56},{72,6... | collective-permute-start | bytes 2856968 | tf_op jit(solution)/shard_map/ppermute | solution.py:20
  239.2 35.0 %collective-permute-start.7 = (f32[30,62,128]{2,1,0:T(8,128)S(1)}, f32[30,62,128]{2,1,0:T(8,128)S(1)}, u32[]{:S(2)}, u32[]{:S(2)}) collective-permute-start(f32[30,62,128]{2,1,0:T(8,128)S(1)} %copy-done.25), channel_id=1, source_target_pairs={{8,0},{16,8},{24,16},{32,24},{40,32},{48,40},{56,48},{64,56},{72,6... | collective-permute-start | bytes 2856968 | tf_op jit(solution)/shard_map/ppermute | solution.py:20
  241.2 43.0 %collective-permute-start.26 = (f32[30,62,128]{2,1,0:T(8,128)S(1)}, f32[30,62,128]{2,1,0:T(8,128)S(1)}, u32[]{:S(2)}, u32[]{:S(2)}) collective-permute-start(f32[30,62,128]{2,1,0:T(8,128)S(1)} %get-tuple-element.61), channel_id=1, source_target_pairs={{0,8},{8,16},{16,24},{24,32},{32,40},{40,48},{48,56},{56,64},{64,7... | collective-permute-start | bytes 2856968 | tf_op jit(solution)/shard_map/ppermute | solution.py:18
  250.1 41.6 %collective-permute-start.27 = (f32[30,62,128]{2,1,0:T(8,128)S(1)}, f32[30,62,128]{2,1,0:T(8,128)S(1)}, u32[]{:S(2)}, u32[]{:S(2)}) collective-permute-start(f32[30,62,128]{2,1,0:T(8,128)S(1)} %get-tuple-element.62), channel_id=1, source_target_pairs={{8,0},{16,8},{24,16},{32,24},{40,32},{48,40},{56,48},{64,56},{72,6... | collective-permute-start | bytes 2856968 | tf_op jit(solution)/shard_map/ppermute | solution.py:20
  256.9 42.4 %collective-permute-start.22 = (f32[30,62,128]{2,1,0:T(8,128)S(1)}, f32[30,62,128]{2,1,0:T(8,128)S(1)}, u32[]{:S(2)}, u32[]{:S(2)}) collective-permute-start(f32[30,62,128]{2,1,0:T(8,128)S(1)} %get-tuple-element.59), channel_id=1, source_target_pairs={{0,8},{8,16},{16,24},{24,32},{32,40},{40,48},{48,56},{56,64},{64,7... | collective-permute-start | bytes 2856968 | tf_op jit(solution)/shard_map/ppermute | solution.py:18
  267.0 32.3 %collective-permute-start.23 = (f32[30,62,128]{2,1,0:T(8,128)S(1)}, f32[30,62,128]{2,1,0:T(8,128)S(1)}, u32[]{:S(2)}, u32[]{:S(2)}) collective-permute-start(f32[30,62,128]{2,1,0:T(8,128)S(1)} %get-tuple-element.60), channel_id=1, source_target_pairs={{8,0},{16,8},{24,16},{32,24},{40,32},{48,40},{56,48},{64,56},{72,6... | collective-permute-start | bytes 2856968 | tf_op jit(solution)/shard_map/ppermute | solution.py:20
  274.3 33.1 %collective-permute-start.18 = (f32[30,62,128]{2,1,0:T(8,128)S(1)}, f32[30,62,128]{2,1,0:T(8,128)S(1)}, u32[]{:S(2)}, u32[]{:S(2)}) collective-permute-start(f32[30,62,128]{2,1,0:T(8,128)S(1)} %get-tuple-element.57), channel_id=1, source_target_pairs={{0,8},{8,16},{16,24},{24,32},{32,40},{40,48},{48,56},{56,64},{64,7... | collective-permute-start | bytes 2856968 | tf_op jit(solution)/shard_map/ppermute | solution.py:18
  384.5 40.3 %collective-permute-start.48 = (f32[48,15,128]{2,1,0:T(8,128)S(1)}, f32[48,15,128]{2,1,0:T(8,128)S(1)}, u32[]{:S(2)}, u32[]{:S(2)}) collective-permute-start(f32[48,15,128]{2,1,0:T(8,128)S(1)} %get-tuple-element.73), channel_id=1, source_target_pairs={{0,1},{1,2},{2,3},{3,4},{4,5},{5,6},{6,7},{8,9},{9,10},{10,11},{11... | collective-permute-start | bytes 1105928 | tf_op jit(solution)/shard_map/ppermute | solution.py:18
  386.4 40.3 %collective-permute-start.49 = (f32[48,15,128]{2,1,0:T(8,128)S(1)}, f32[48,15,128]{2,1,0:T(8,128)S(1)}, u32[]{:S(2)}, u32[]{:S(2)}) collective-permute-start(f32[48,15,128]{2,1,0:T(8,128)S(1)} %get-tuple-element.74), channel_id=1, source_target_pairs={{1,0},{2,1},{3,2},{4,3},{5,4},{6,5},{7,6},{9,8},{10,9},{11,10},{12... | collective-permute-start | bytes 1105928 | tf_op jit(solution)/shard_map/ppermute | solution.py:20
  415.2 41.8 %collective-permute-start.36 = (f32[48,15,128]{2,1,0:T(8,128)S(1)}, f32[48,15,128]{2,1,0:T(8,128)S(1)}, u32[]{:S(2)}, u32[]{:S(2)}) collective-permute-start(f32[48,15,128]{2,1,0:T(8,128)S(1)} %get-tuple-element.67), channel_id=1, source_target_pairs={{0,1},{1,2},{2,3},{3,4},{4,5},{5,6},{6,7},{8,9},{9,10},{10,11},{11... | collective-permute-start | bytes 1105928 | tf_op jit(solution)/shard_map/ppermute | solution.py:18
  417.4 41.6 %collective-permute-start.37 = (f32[48,15,128]{2,1,0:T(8,128)S(1)}, f32[48,15,128]{2,1,0:T(8,128)S(1)}, u32[]{:S(2)}, u32[]{:S(2)}) collective-permute-start(f32[48,15,128]{2,1,0:T(8,128)S(1)} %get-tuple-element.68), channel_id=1, source_target_pairs={{1,0},{2,1},{3,2},{4,3},{5,4},{6,5},{7,6},{9,8},{10,9},{11,10},{12... | collective-permute-start | bytes 1105928 | tf_op jit(solution)/shard_map/ppermute | solution.py:20
  454.6 74.9 %collective-permute-start.34 = (f32[30,62,128]{2,1,0:T(8,128)S(1)}, f32[30,62,128]{2,1,0:T(8,128)S(1)}, u32[]{:S(2)}, u32[]{:S(2)}) collective-permute-start(f32[30,62,128]{2,1,0:T(8,128)S(1)} %get-tuple-element.37), channel_id=1, source_target_pairs={{0,8},{8,16},{16,24},{24,32},{32,40},{40,48},{48,56},{56,64},{64,7... | collective-permute-start | bytes 2856968 | tf_op jit(solution)/shard_map/ppermute | solution.py:18
  467.1 62.4 %collective-permute-start.35 = (f32[30,62,128]{2,1,0:T(8,128)S(1)}, f32[30,62,128]{2,1,0:T(8,128)S(1)}, u32[]{:S(2)}, u32[]{:S(2)}) collective-permute-start(f32[30,62,128]{2,1,0:T(8,128)S(1)} %get-tuple-element.38), channel_id=1, source_target_pairs={{8,0},{16,8},{24,16},{32,24},{40,32},{48,40},{56,48},{64,56},{72,6... | collective-permute-start | bytes 2856968 | tf_op jit(solution)/shard_map/ppermute | solution.py:20
  504.2 33.3 %collective-permute-start.38 = (f32[30,62,128]{2,1,0:T(8,128)S(1)}, f32[30,62,128]{2,1,0:T(8,128)S(1)}, u32[]{:S(2)}, u32[]{:S(2)}) collective-permute-start(f32[30,62,128]{2,1,0:T(8,128)S(1)} %get-tuple-element.39), channel_id=1, source_target_pairs={{0,8},{8,16},{16,24},{24,32},{32,40},{40,48},{48,56},{56,64},{64,7... | collective-permute-start | bytes 2856968 | tf_op jit(solution)/shard_map/ppermute | solution.py:18
  (144 other events, 2019.4 us)
